TPU v7x, 512 devices: a whole 4x4x16 slice. The times are simulated.
512 devices in a mesh: dp: 2 (over z_hi), fsdp: 16 (over z_lo, core), tile: 16 (over y, x).
Axes of the slice: x: 4, y: 4, z: 16 (z_hi: 2, z_lo: 8; z = z_hi * 8 + z_lo), core: 2. Of those that a mesh axis runs over, the one named last changes fastest.
Arguments:
- tokens: bfloat16 [32, 8, 512, 1536], P(('dp', 'fsdp'), None, 'tile'), may hold values from -6 to 6
- norm_gain: float32 [1536], replicated, may hold values from 0.25 to 1.75
- query_key_value_weight: bfloat16 [1536, 2304], P('fsdp'), may hold values from -5 to 5
- out_weight: bfloat16 [768, 1536], P('fsdp'), may hold values from -0.21875 to 0.21875
- head_weight: bfloat16 [1536, 320], P('fsdp'), may hold values from -0.15625 to 0.15625
- coarse: float32 [32, 20, 8, 512], P(('dp', 'fsdp'), None, None, 'tile'), may hold values from -36 to 36
- grad_fine: float32 [32, 20, 32, 2048], P(('dp', 'fsdp'), None, None, 'tile'), may hold values from -0.6 to 0.6
Outputs:
- fine_grid: float32 [32, 20, 32, 2048], P(('dp', 'fsdp'), None, None, 'tile')
- grad_tokens: bfloat16 [32, 8, 512, 1536], P(('dp', 'fsdp'), None, 'tile')
- grad_head: float32 [1536, 320], P('fsdp')
All inputs are finite; a program needn't handle non-finite values.
Results may differ from a plain program's by a relative error of at most 0.0059.
Values may be sent and summed in bfloat16 or wider, within the bound.
No kernel may reach another device: no remote copies, remote signals or barrier semaphores. Data moves between devices by JAX's collectives and lax.ppermute only.
A program may use at most 64 MiB of HBM per device.

v0:
```python
import jax
import jax.numpy as jnp
from jax import lax
from jax.sharding import Mesh
from jax.sharding import PartitionSpec as P

D = 1536
HEADS = 8
HEAD_DIM = 96
VARS = 20
MARGIN = 8
INNER = 768
HEAD_OUT = 320
EPSILON = 1e-05


def with_halo(shard, sides, width):
    for axis, dim in sides:
        devices, length = (lax.axis_size(axis), shard.shape[dim])
        up = [(i, (i + 1) % devices) for i in range(devices)]
        down = [(j, i) for i, j in up]
        last = lax.slice_in_dim(shard, length - width, length, axis=dim)
        leading = lax.slice_in_dim(shard, 0, width, axis=dim)
        before = lax.ppermute(last, axis, up)
        after = lax.ppermute(leading, axis, down)
        shard = jnp.concatenate([before, shard, after], axis=dim)
    return shard


def from_behind(value, axis, steps):
    count = lax.axis_size(axis)
    pairs = [(source, (source + steps) % count) for source in range(count)]
    return lax.ppermute(value, axis, pairs)


def layer_norm(values):
    average = jnp.mean(values, axis=-1, keepdims=True)
    centred = values - average
    variance = jnp.mean(centred * centred, axis=-1, keepdims=True)
    inverse_dev = lax.rsqrt(variance + EPSILON)
    return (centred * inverse_dev, inverse_dev)


def norm_backward(grad_normed, standard, inverse_dev, norm_gain):
    grad_standard = grad_normed * norm_gain
    first_mean = jnp.mean(grad_standard, axis=-1, keepdims=True)
    second_mean = jnp.mean(grad_standard * standard, axis=-1, keepdims=True)
    return inverse_dev * (grad_standard - first_mean - standard * second_mean)


def attend_forward(queries, keys_values):
    query_count = queries.shape[0]
    key_count = keys_values.shape[0]
    score_scale = HEAD_DIM ** (-0.5)
    query_heads = queries.reshape(query_count, HEADS, HEAD_DIM)
    key_heads = keys_values[:, :INNER].reshape(key_count, HEADS, HEAD_DIM)
    value_heads = keys_values[:, INNER:].reshape(key_count, HEADS, HEAD_DIM)
    scores = (
        jnp.einsum("qhd,khd->hqk", query_heads, key_heads, preferred_element_type=jnp.float32)
        * score_scale
    )
    biggest = jnp.max(scores, axis=-1, keepdims=True)
    exponent = jnp.exp(scores - biggest)
    softmax_out = exponent / jnp.sum(exponent, axis=-1, keepdims=True)
    softmax_low = softmax_out.astype(jnp.bfloat16)
    attended = jnp.einsum(
        "hqk,khd->qhd", softmax_low, value_heads, preferred_element_type=jnp.float32
    )
    return (attended.astype(jnp.bfloat16).reshape(query_count, INNER), softmax_out)


def attend_backward(softmax_out, queries, keys_values, grad_attended):
    query_count = queries.shape[0]
    key_count = keys_values.shape[0]
    score_scale = HEAD_DIM ** (-0.5)
    query_heads = queries.reshape(query_count, HEADS, HEAD_DIM)
    key_heads = keys_values[:, :INNER].reshape(key_count, HEADS, HEAD_DIM)
    value_heads = keys_values[:, INNER:].reshape(key_count, HEADS, HEAD_DIM)
    grad_heads = grad_attended.reshape(query_count, HEADS, HEAD_DIM)
    softmax_low = softmax_out.astype(jnp.bfloat16)
    grad_values = jnp.einsum(
        "hqk,qhd->khd", softmax_low, grad_heads, preferred_element_type=jnp.float32
    )
    grad_weights = jnp.einsum(
        "qhd,khd->hqk", grad_heads, value_heads, preferred_element_type=jnp.float32
    )
    weighted = jnp.sum(softmax_out * grad_weights, axis=-1, keepdims=True)
    grad_scores = (softmax_out * (grad_weights - weighted)).astype(jnp.bfloat16)
    grad_queries = (
        jnp.einsum("hqk,khd->qhd", grad_scores, key_heads, preferred_element_type=jnp.float32)
        * score_scale
    )
    grad_keys = (
        jnp.einsum("hqk,qhd->khd", grad_scores, query_heads, preferred_element_type=jnp.float32)
        * score_scale
    )
    pair_gradient_rows = jnp.concatenate(
        [grad_keys.reshape(key_count, INNER), grad_values.reshape(key_count, INNER)], axis=1
    )
    return (grad_queries.astype(jnp.bfloat16).reshape(query_count, INNER), pair_gradient_rows)


def interp_weights(fine_index):
    coarse_cell = fine_index // 4
    phase_index = fine_index % 4
    lower_shift = (phase_index < 2).astype(jnp.int32)
    upper_weight = (2 * phase_index - 3 + 8 * lower_shift).astype(jnp.float32) / 8.0
    return (coarse_cell - lower_shift, upper_weight)


def build_matrix(lower_cell, upper_cell, upper_weight, count):
    columns = jnp.arange(count, dtype=jnp.int32)
    lower_part = jnp.where(
        columns[None, :] == lower_cell[:, None], 1.0 - upper_weight[:, None], 0.0
    )
    upper_portion = jnp.where(columns[None, :] == upper_cell[:, None], upper_weight[:, None], 0.0)
    return lower_part + upper_portion


def contract_last(left_side, right_side):
    return lax.dot_general(
        left_side, right_side, (((1,), (1,)), ((), ())), preferred_element_type=jnp.float32
    )


ZS = 8
CORES = 2
YS = 4
XS = 4
FSDP = ("z", "c")
TILE = ("y", "x")
HALF_QKV = 1152
HALF_OUT = 768


def gather_weights(qkv, out_w, head_w):
    half = lax.axis_index("dp")
    qkv_half = lax.dynamic_slice_in_dim(qkv, half * HALF_QKV, HALF_QKV, 1)
    out_half = lax.dynamic_slice_in_dim(out_w, half * HALF_OUT, HALF_OUT, 1)
    out_half = jnp.concatenate([out_half[:, :384], out_half[:, 384:]], axis=0)
    head_half = lax.dynamic_slice_in_dim(head_w, half * 160, 160, 1)
    packed = jnp.concatenate([qkv_half, out_half, head_half], axis=1)
    full = lax.all_gather(packed, ("dp",) + FSDP, axis=0, tiled=True)
    full = full.reshape(2, D, 1696)
    full_qkv = jnp.concatenate([full[0, :, :HALF_QKV], full[1, :, :HALF_QKV]], axis=1)
    out_part = full[:, :, HALF_QKV:1536].reshape(2, 16, 2, 48, 384)
    full_out = out_part.transpose(1, 3, 0, 2, 4).reshape(INNER, D)
    full_head = jnp.concatenate([full[0, :, 1536:], full[1, :, 1536:]], axis=1)
    return (full_qkv, full_out, full_head)


def reduce_head(head_term):
    core = lax.axis_index("c")
    parts = head_term.reshape(ZS, CORES, 96, HEAD_OUT)
    own = lax.dynamic_index_in_dim(parts, core, 1, keepdims=False)
    other = lax.dynamic_index_in_dim(parts, 1 - core, 1, keepdims=False)
    pair = own + lax.ppermute(other, "c", [(0, 1), (1, 0)])
    pieces = pair.reshape(ZS, 16, 6, HEAD_OUT).transpose(1, 0, 2, 3).astype(jnp.bfloat16)
    pieces = lax.all_to_all(pieces, TILE, 0, 0, tiled=True)
    over_tile = jnp.sum(pieces.astype(jnp.float32), axis=0)
    both = jnp.broadcast_to(over_tile[None], (2, ZS, 6, HEAD_OUT)).reshape(2 * ZS, 6, HEAD_OUT)
    both = lax.all_to_all(both, ("dp", "z"), 0, 0, tiled=True)
    total = jnp.sum(both, axis=0)
    spread = jnp.broadcast_to(total[None], (16, 6, HEAD_OUT))
    return lax.all_to_all(spread, TILE, 0, 0, tiled=True).reshape(96, HEAD_OUT)


def shards(tokens, norm_gain, query_key_value_weight, out_weight, head_weight, coarse, grad_fine):
    lat_rows = tokens.shape[1]
    lon_cols = tokens.shape[2]
    row_count = lat_rows * lon_cols
    flattened_rows = tokens[0].reshape(row_count, D).astype(jnp.float32)
    standard, inverse_dev = layer_norm(flattened_rows)
    normed = (standard * norm_gain).astype(jnp.bfloat16)
    full_qkv, full_out, full_head = gather_weights(query_key_value_weight, out_weight, head_weight)
    projected = jnp.dot(normed, full_qkv, preferred_element_type=jnp.float32).astype(jnp.bfloat16)
    queries = projected[:, :INNER]
    pairs_local = projected[:, INNER:]
    margin_pairs = with_halo(
        pairs_local.reshape(lat_rows, lon_cols, 2 * INNER), ((TILE, 1),), MARGIN
    )
    keys_values = margin_pairs.reshape(lat_rows * (lon_cols + 2 * MARGIN), 2 * INNER)
    attended, softmax_out = attend_forward(queries, keys_values)
    mixed_out = jnp.dot(attended, full_out, preferred_element_type=jnp.float32)
    hidden = (flattened_rows + mixed_out).astype(jnp.bfloat16)
    head_out = jnp.dot(hidden, full_head, preferred_element_type=jnp.float32)
    fine_head = (
        head_out.reshape(lat_rows, lon_cols, VARS, 4, 4)
        .transpose(2, 0, 3, 1, 4)
        .reshape(VARS, 4 * lat_rows, 4 * lon_cols)
    )
    coarse_padded_grid = with_halo(coarse[0], ((TILE, 2),), 1)
    lat_lower, lat_upper_weight = interp_weights(jnp.arange(4 * lat_rows, dtype=jnp.int32))
    latitude_matrix = build_matrix(
        jnp.clip(lat_lower, 0, lat_rows - 1),
        jnp.clip(lat_lower + 1, 0, lat_rows - 1),
        lat_upper_weight,
        lat_rows,
    )
    lon_lower, lon_upper_weight = interp_weights(jnp.arange(4 * lon_cols, dtype=jnp.int32))
    lon_matrix = build_matrix(lon_lower + 1, lon_lower + 2, lon_upper_weight, lon_cols + 2)
    incomplete_grid = jnp.einsum(
        "lj,kji->kli", latitude_matrix, coarse_padded_grid, precision=lax.Precision.HIGHEST
    )
    residual = jnp.einsum(
        "vrb,cb->vrc", incomplete_grid, lon_matrix, precision=lax.Precision.HIGHEST
    )
    fine_grid = fine_head + residual
    grad_rows = (
        grad_fine[0]
        .reshape(VARS, lat_rows, 4, lon_cols, 4)
        .transpose(1, 3, 0, 2, 4)
        .reshape(row_count, HEAD_OUT)
    )
    grad_rows = grad_rows.astype(jnp.bfloat16)
    head_term = lax.dot_general(
        hidden, grad_rows, (((0,), (0,)), ((), ())), preferred_element_type=jnp.float32
    )
    grad_head = reduce_head(head_term)
    grad_hidden = contract_last(grad_rows, full_head)
    grad_attended = contract_last(grad_hidden.astype(jnp.bfloat16), full_out).astype(jnp.bfloat16)
    grad_queries, pair_gradient_rows = attend_backward(
        softmax_out, queries, keys_values, grad_attended
    )
    pair_gradient_rows = pair_gradient_rows.reshape(lat_rows, lon_cols + 2 * MARGIN, 2 * INNER)
    from_left = from_behind(pair_gradient_rows[:, lon_cols + MARGIN :], TILE, 1)
    from_right = from_behind(pair_gradient_rows[:, :MARGIN], TILE, -1)
    own_cells = pair_gradient_rows[:, MARGIN : MARGIN + lon_cols]
    own_cells = own_cells + jnp.pad(from_left, ((0, 0), (0, lon_cols - MARGIN), (0, 0)))
    own_cells = own_cells + jnp.pad(from_right, ((0, 0), (lon_cols - MARGIN, 0), (0, 0)))
    grad_all = jnp.concatenate(
        [grad_queries, own_cells.reshape(row_count, 2 * INNER).astype(jnp.bfloat16)], axis=1
    )
    grad_normed = contract_last(grad_all, full_qkv)
    grad_input = grad_hidden + norm_backward(grad_normed, standard, inverse_dev, norm_gain)
    grad_tokens = grad_input.astype(jnp.bfloat16).reshape(1, lat_rows, lon_cols, D)
    return (fine_grid[None], grad_tokens, grad_head)


def solution(mesh):
    fine_mesh = Mesh(mesh.devices.reshape(2, ZS, CORES, YS, XS), ("dp", "z", "c", "y", "x"))
    samples = ("dp", "z", "c")
    placed = (
        P(samples, None, TILE, None),
        P(),
        P(FSDP, None),
        P(FSDP, None),
        P(FSDP, None),
        P(samples, None, None, TILE),
        P(samples, None, None, TILE),
    )
    return jax.shard_map(
        shards,
        mesh=fine_mesh,
        in_specs=placed,
        out_specs=(P(samples, None, None, TILE), P(samples, None, TILE, None), P(FSDP, None)),
        check_vma=False,
    )
```

profile of v0, /device:TPU:32, one launch (start us, length us, event | category | flops | bytes accessed | tf_op | source)
XLA Modules:
  0.0 268.6 jit_solution(15269680158934245788)
XLA Ops:
  10.0 3.4 %collective-permute-start.2 = (f32[20,8,1]{2,1,0:T(8,128)S(1)}, f32[20,8,1]{2,1,0:T(8,128)S(1)}, u32[]{:S(2)}, u32[]{:S(2)}) collective-permute-start(f32[20,8,1]{2,1,0:T(8,128)S(1)} %get-tuple-element.17), channel_id=1, source_target_pairs={{0,1},{1,2},{2,3},{3,4},{4,5},{5,6},{6,7},{7,8},{8,9},{9,10},{10,1... | collective-permute-start | bytes 1928 | tf_op jit(solution)/shard_map/ppermute | solution.py:24
  13.4 5.8 %collective-permute-start.3 = (f32[20,8,1]{2,1,0:T(8,128)S(1)}, f32[20,8,1]{2,1,0:T(8,128)S(1)}, u32[]{:S(2)}, u32[]{:S(2)}) collective-permute-start(f32[20,8,1]{2,1,0:T(8,128)S(1)} %get-tuple-element.18), channel_id=1, source_target_pairs={{1,0},{2,1},{3,2},{4,3},{5,4},{6,5},{7,6},{8,7},{9,8},{10,9},{11,1... | collective-permute-start | bytes 1928 | tf_op jit(solution)/shard_map/ppermute | solution.py:25
  27.0 70.3 %all-gather.2.cloned.1.call-done = bf16[3072,1696]{1,0:T(8,128)(2,1)} async-done(((bf16[96,1696]{1,0:T(8,128)(2,1)}), bf16[3072,1696]{1,0:T(8,128)(2,1)}) %all-gather.2.cloned.1.call-update) | async-done | bytes 10420240 | tf_op jit(solution)/shard_map/all_gather | solution.py:143
  97.3 2.6 slice_bitcast_fusion.3
  101.9 3.7 %slice_bitcast_fusion.1 = (bf16[1536,1152]{1,0:T(8,128)(2,1)S(1)}, bf16[1536,1152]{1,0:T(8,128)(2,1)S(1)}) fusion(bf16[2,1536,1696]{2,1,0:T(8,128)(2,1)} %bitcast.108), kind=kLoop, calls=%fused_computation.6 | loop fusion | bytes 14155776 | tf_op jit(solution)/shard_map/squeeze | solution.py:145
  105.6 3.8 %fusion.3 = bf16[256,2304]{1,0:T(8,128)(2,1)S(1)} fusion(bf16[256,1536]{1,0:T(8,128)(2,1)S(1)} %multiply_convert_fusion.1, bf16[1536,1152]{1,0:T(8,128)(2,1)S(1)} %get-tuple-element.8, bf16[1536,1152]{1,0:T(8,128)(2,1)S(1)} %get-tuple-element.7), kind=kOutput, calls=%fused_computation.4 | convolution fusion | flops 1826684928 | bytes 9043968 | tf_op jit(solution)/shard_map/dot_general | solution.py:176
  111.1 3.7 %copy.76 = bf16[16,48,2,2,384]{4,3,2,1,0:T(2,128)(2,1)} copy(bf16[16,48,2,2,384]{4,1,3,0,2:T(8,128)(2,1)S(1)} %bitcast.109) | data formatting | bytes 4718592 | tf_op jit(solution)/shard_map/transpose | solution.py:147
  114.8 5.3 %reshape.212 = bf16[768,1536]{1,0:T(8,128)(2,1)S(1)} reshape(bf16[16,48,2,2,384]{4,3,2,1,0:T(2,128)(2,1)} %copy.76) | data formatting | bytes 4718592 | tf_op jit(solution)/shard_map/reshape | solution.py:147
  123.1 3.4 %collective-permute-start = (bf16[8,8,1536]{2,1,0:T(8,128)(2,1)}, bf16[8,8,1536]{2,1,0:T(8,128)(2,1)}, u32[]{:S(2)}, u32[]{:S(2)}) collective-permute-start(bf16[8,8,1536]{2,1,0:T(8,128)(2,1)} %get-tuple-element.13), channel_id=1, source_target_pairs={{0,1},{1,2},{2,3},{3,4},{4,5},{5,6},{6,7},{7,8},{8,9},{9,10},{10,1... | collective-permute-start | bytes 589832 | tf_op jit(solution)/shard_map/ppermute | solution.py:24
  126.4 6.0 %collective-permute-start.1 = (bf16[8,8,1536]{2,1,0:T(8,128)(2,1)}, bf16[8,8,1536]{2,1,0:T(8,128)(2,1)}, u32[]{:S(2)}, u32[]{:S(2)}) collective-permute-start(bf16[8,8,1536]{2,1,0:T(8,128)(2,1)} %get-tuple-element.14), channel_id=1, source_target_pairs={{1,0},{2,1},{3,2},{4,3},{5,4},{6,5},{7,6},{8,7},{9,8},{10,9},{11,1... | collective-permute-start | bytes 589832 | tf_op jit(solution)/shard_map/ppermute | solution.py:25
  132.4 2.1 convolution_bitcast_fusion
  141.6 2.1 copy.92
  143.8 2.1 copy.91
  145.9 3.9 %fusion.68 = (f32[8,256]{1,0:T(8,128)S(1)}, f32[8,256,384]{2,1,0:T(8,128)}) fusion(bf16[256,8,96]{0,2,1:T(8,128)(2,1)S(1)} %bitcast.117, bf16[384,8,96]{0,2,1:T(8,128)(2,1)} %bitcast.111), kind=kOutput, calls=%fused_computation.133 | convolution fusion | flops 153354624 | bytes 4136960 | tf_op jit(solution)/shard_map/sub | solution.py:63
  149.8 2.9 %convolution_convert_fusion.1 = bf16[8,96,256]{2,1,0:T(8,128)(2,1)S(1)} fusion(bf16[384,8,96]{0,2,1:T(8,128)(2,1)} %bitcast.127, f32[8,256,384]{2,1,0:T(8,128)} %get-tuple-element.20, f32[8,256]{1,0:T(8,128)S(1)} %get-tuple-element.19), kind=kOutput, calls=%fused_computation.33 | convolution fusion | flops 152764416 | bytes 4136960 | tf_op jit(solution)/shard_map/hqk,khd->qhd/dot_general | solution.py:66
  161.1 2.4 copy.85
  170.7 3.1 %copy.77 = f32[8,32,20,4,4]{2,4,1,3,0:T(4,128)} copy(f32[8,32,20,4,4]{1,0,4,3,2:T(8,128)} %reshape.213) | data formatting | bytes 655360 | tf_op jit(solution)/shard_map/reshape | solution.py:188
  173.7 3.0 %copy.78 = f32[20,32,128]{2,1,0:T(8,128)} copy(f32[20,32,128]{0,2,1:T(8,128)} %bitcast.110) | data formatting | bytes 655360 | tf_op jit(solution)/shard_map/reshape | solution.py:190
  176.7 3.0 %copy.83 = f32[384,8,96]{2,1,0:T(8,128)} copy(f32[384,8,96]{0,2,1:T(8,128)} %convolution_bitcast_fusion.1) | data formatting | bytes 2359296 | tf_op jit(solution)/shard_map/hqk,qhd->khd/transpose | solution.py:81
  179.7 2.8 %concatenate.36 = f32[8,48,768]{2,1,0:T(8,128)} reshape(f32[384,8,96]{2,1,0:T(8,128)} %copy.83) | data formatting | bytes 2359296 | tf_op jit(solution)/shard_map/concatenate | solution.py:97
  183.5 3.0 %copy.82 = f32[384,8,96]{2,1,0:T(8,128)} copy(f32[384,8,96]{0,2,1:T(8,128)} %fusion.13) | data formatting | bytes 2359296 | tf_op jit(solution)/shard_map/mul | solution.py:94
  186.5 2.7 concatenate.35
  195.3 7.5 %collective-permute-start.5 = (f32[8,8,1536]{2,1,0:T(8,128)}, f32[8,8,1536]{2,1,0:T(8,128)}, u32[]{:S(2)}, u32[]{:S(2)}) collective-permute-start(f32[8,8,1536]{2,1,0:T(8,128)} %get-tuple-element.10), channel_id=1, source_target_pairs={{0,15},{1,0},{2,1},{3,2},{4,3},{5,4},{6,5},{7,6},{8,7},{9,8},{10,9... | collective-permute-start | bytes 1179656 | tf_op jit(solution)/shard_map/ppermute | solution.py:33
  206.4 4.2 %all-to-all-start = ((bf16[16,8,6,320]{3,1,2,0:T(8,128)(2,1)}), bf16[16,8,6,320]{3,1,2,0:T(8,128)(2,1)}, u32[]{:S(2)}, u32[]{:S(2)}) async-start(bf16[16,8,6,320]{3,1,2,0:T(8,128)(2,1)} %bitcast.121), calls=%async_computation | async-start | bytes 1179648 | tf_op jit(solution)/shard_map/all_to_all | solution.py:159
  212.0 2.0 fusion.10
  214.0 9.3 %all-to-all-done = bf16[16,8,6,320]{3,1,2,0:T(8,128)(2,1)} async-done(((bf16[16,8,6,320]{3,1,2,0:T(8,128)(2,1)}), bf16[16,8,6,320]{3,1,2,0:T(8,128)(2,1)}, u32[]{:S(2)}, u32[]{:S(2)}) %all-to-all-start) | async-done | bytes 491552 | tf_op jit(solution)/shard_map/all_to_all | solution.py:159
  225.2 7.7 %all-to-all-start.1 = ((f32[16,6,320]{2,1,0:T(8,128)}), f32[16,6,320]{2,1,0:T(8,128)S(1)}, u32[]{:S(2)}, u32[]{:S(2)}) async-start(f32[16,6,320]{2,1,0:T(8,128)} %bitcast.39), calls=%async_computation.1 | async-start | bytes 393216 | tf_op jit(solution)/shard_map/all_to_all | solution.py:162
  232.9 6.8 %fusion.63 = (f32[256]{0:T(256)S(1)}, f32[256]{0:T(256)S(1)}, f32[256,1536]{1,0:T(8,128)}) fusion(f32[256]{0:T(256)S(1)} %rsqrt.12, f32[256]{0:T(256)S(1)} %div.51, bf16[1,8,32,1536]{3,2,1,0:T(8,128)(2,1)S(1)} %copy-done.2, f32[1536]{0:T(1024)S(1)} %copy-done.24, bf16[1536,1152]{1,0:T(8,128)(2,1)} %copy-done.11, bf16[1536,1152]{1,0:T(8,128)(2,1)} %copy-done.10, ...), kind=kOutput, calls=%fused_computation.128 | convolution fusion | flops 1831206400 | bytes 10627072 | tf_op jit(solution)/shard_map/dot_general | solution.py:121
  239.7 8.8 %all-to-all-done.1 = f32[16,6,320]{2,1,0:T(8,128)S(1)} async-done(((f32[16,6,320]{2,1,0:T(8,128)}), f32[16,6,320]{2,1,0:T(8,128)S(1)}, u32[]{:S(2)}, u32[]{:S(2)}) %all-to-all-start.1) | async-done | bytes 122912 | tf_op jit(solution)/shard_map/all_to_all | solution.py:162
  249.2 3.5 %all-to-all-start.2 = ((f32[16,6,320]{2,1,0:T(8,128)}), f32[16,6,320]{2,1,0:T(8,128)S(1)}, u32[]{:S(2)}, u32[]{:S(2)}) async-start(f32[16,6,320]{2,1,0:T(8,128)} %broadcast_in_dim.80), calls=%async_computation.2 | async-start | bytes 393216 | tf_op jit(solution)/shard_map/all_to_all | solution.py:165
  252.8 2.9 %add_convert_fusion = bf16[256,1536]{1,0:T(8,128)(2,1)} fusion(f32[256,1536]{1,0:T(8,128)S(1)} %copy-done.4, f32[256,1536]{1,0:T(8,128)} %get-tuple-element.23, bf16[1,8,32,1536]{3,2,1,0:T(8,128)(2,1)S(1)} %copy-done.2, f32[256]{0:T(256)S(1)} %get-tuple-element.32, f32[256]{0:T(256)S(1)} %get-tuple-element.33, f32[256]{0:T(256)S(1)} %rsqrt.12, f32[256]{0:T(256)S(1)} %div.51), kind=kLoop, calls=%fused_computation.21 | loop fusion | flops 3538944 | bytes 4722688 | tf_op jit(solution)/shard_map/convert_element_type | solution.py:236
  255.7 5.4 %all-to-all-done.2 = f32[16,6,320]{2,1,0:T(8,128)S(1)} async-done(((f32[16,6,320]{2,1,0:T(8,128)}), f32[16,6,320]{2,1,0:T(8,128)S(1)}, u32[]{:S(2)}, u32[]{:S(2)}) %all-to-all-start.2) | async-done | bytes 122912 | tf_op jit(solution)/shard_map/all_to_all | solution.py:165
  (124 shorter events, 54.9 us)
Async XLA Ops:
  7.2 12.0 %copy-start.22 = (f32[1,20,32,128]{3,2,1,0:T(8,128)S(1)}, f32[1,20,32,128]{3,2,1,0:T(8,128)}, u32[]{:S(2)}) copy-start(f32[1,20,32,128]{3,2,1,0:T(8,128)} %param.13) | copy-start | bytes 983044
  7.2 90.1 %all-gather.2.cloned.1.call-start = ((), (), s32[]{:S(2)}) async-start(), calls=%async_computation.3 | async-start | bytes 11354112 | tf_op jit(solution)/shard_map/all_gather | solution.py:143
  10.0 15.7 %collective-permute-start.2 = (f32[20,8,1]{2,1,0:T(8,128)S(1)}, f32[20,8,1]{2,1,0:T(8,128)S(1)}, u32[]{:S(2)}, u32[]{:S(2)}) collective-permute-start(f32[20,8,1]{2,1,0:T(8,128)S(1)} %get-tuple-element.17), channel_id=1, source_target_pairs={{0,1},{1,2},{2,3},{3,4},{4,5},{5,6},{6,7},{7,8},{8,9},{9,10},{10,1... | collective-permute-start | bytes 1928 | tf_op jit(solution)/shard_map/ppermute | solution.py:24
  13.4 12.3 %collective-permute-start.3 = (f32[20,8,1]{2,1,0:T(8,128)S(1)}, f32[20,8,1]{2,1,0:T(8,128)S(1)}, u32[]{:S(2)}, u32[]{:S(2)}) collective-permute-start(f32[20,8,1]{2,1,0:T(8,128)S(1)} %get-tuple-element.18), channel_id=1, source_target_pairs={{1,0},{2,1},{3,2},{4,3},{5,4},{6,5},{7,6},{8,7},{9,8},{10,9},{11,1... | collective-permute-start | bytes 1928 | tf_op jit(solution)/shard_map/ppermute | solution.py:25
  19.8 3.7 %copy-start.2 = (bf16[1,8,32,1536]{3,2,1,0:T(8,128)(2,1)S(1)}, bf16[1,8,32,1536]{3,2,1,0:T(8,128)(2,1)}, u32[]{:S(2)}) copy-start(bf16[1,8,32,1536]{3,2,1,0:T(8,128)(2,1)} %param.7) | copy-start | bytes 2359300
  21.3 4.2 %copy-start.23 = (f32[1536]{0:T(1024)S(1)}, f32[1536]{0:T(1024)}, u32[]{:S(2)}) copy-start(f32[1536]{0:T(1024)} %param.8) | copy-start | bytes 18436
  105.6 3.8 %copy-start.10 = (bf16[1536,1152]{1,0:T(8,128)(2,1)}, bf16[1536,1152]{1,0:T(8,128)(2,1)S(1)}, u32[]{:S(2)}) copy-start(bf16[1536,1152]{1,0:T(8,128)(2,1)S(1)} %get-tuple-element.7) | copy-start | bytes 10616836
  105.6 3.8 %copy-start.11 = (bf16[1536,1152]{1,0:T(8,128)(2,1)}, bf16[1536,1152]{1,0:T(8,128)(2,1)S(1)}, u32[]{:S(2)}) copy-start(bf16[1536,1152]{1,0:T(8,128)(2,1)S(1)} %get-tuple-element.8) | copy-start | bytes 10616836
  123.1 16.1 %collective-permute-start = (bf16[8,8,1536]{2,1,0:T(8,128)(2,1)}, bf16[8,8,1536]{2,1,0:T(8,128)(2,1)}, u32[]{:S(2)}, u32[]{:S(2)}) collective-permute-start(bf16[8,8,1536]{2,1,0:T(8,128)(2,1)} %get-tuple-element.13), channel_id=1, source_target_pairs={{0,1},{1,2},{2,3},{3,4},{4,5},{5,6},{6,7},{7,8},{8,9},{9,10},{10,1... | collective-permute-start | bytes 589832 | tf_op jit(solution)/shard_map/ppermute | solution.py:24
  126.4 12.7 %collective-permute-start.1 = (bf16[8,8,1536]{2,1,0:T(8,128)(2,1)}, bf16[8,8,1536]{2,1,0:T(8,128)(2,1)}, u32[]{:S(2)}, u32[]{:S(2)}) collective-permute-start(bf16[8,8,1536]{2,1,0:T(8,128)(2,1)} %get-tuple-element.14), channel_id=1, source_target_pairs={{1,0},{2,1},{3,2},{4,3},{5,4},{6,5},{7,6},{8,7},{9,8},{10,9},{11,1... | collective-permute-start | bytes 589832 | tf_op jit(solution)/shard_map/ppermute | solution.py:25
  149.8 3.0 %copy-start.5 = (f32[8,256,384]{2,1,0:T(8,128)S(1)}, f32[8,256,384]{2,1,0:T(8,128)}, u32[]{:S(2)}) copy-start(f32[8,256,384]{2,1,0:T(8,128)} %get-tuple-element.20) | copy-start | bytes 9437188
  149.8 3.1 %copy-start.21 = (bf16[256,768]{0,1:T(8,128)(2,1)S(1)}, bf16[256,768]{0,1:T(8,128)(2,1)}, u32[]{:S(2)}) copy-start(bf16[256,768]{0,1:T(8,128)(2,1)} %copy.81) | copy-start | bytes 1179652
  165.1 3.1 %copy-start.12 = (bf16[1536,160]{1,0:T(8,128)(2,1)S(1)}, bf16[1536,160]{1,0:T(8,128)(2,1)}, u32[]{:S(2)}) copy-start(bf16[1536,160]{1,0:T(8,128)(2,1)} %get-tuple-element.5) | copy-start | bytes 1474564
  165.2 3.1 %copy-start.13 = (bf16[1536,160]{1,0:T(8,128)(2,1)S(1)}, bf16[1536,160]{1,0:T(8,128)(2,1)}, u32[]{:S(2)}) copy-start(bf16[1536,160]{1,0:T(8,128)(2,1)} %get-tuple-element.6) | copy-start | bytes 1474564
  165.2 3.1 %copy-start.14 = (bf16[256,1536]{1,0:T(8,128)(2,1)S(1)}, bf16[256,1536]{1,0:T(8,128)(2,1)}, u32[]{:S(2)}) copy-start(bf16[256,1536]{1,0:T(8,128)(2,1)} %fusion.8) | copy-start | bytes 2359300
  166.3 37.7 %collective-permute-start.6 = (f32[8,96,320]{2,1,0:T(8,128)}, f32[8,96,320]{2,1,0:T(8,128)}, u32[]{:S(2)}, u32[]{:S(2)}) collective-permute-start(f32[8,96,320]{2,1,0:T(8,128)} %dynamic-slice_bitcast_fusion), channel_id=1, source_target_pairs={{0,16},{16,0},{1,17},{17,1},{2,18},{18,2},{3,19},{19,3},{4,20},{20... | collective-permute-start | bytes 2949128 | tf_op jit(solution)/shard_map/ppermute | solution.py:157
  179.7 2.8 %copy-start.15 = (bf16[8,96,256]{2,1,0:T(8,128)(2,1)S(1)}, bf16[8,96,256]{2,1,0:T(8,128)(2,1)}, u32[]{:S(2)}) copy-start(bf16[8,96,256]{2,1,0:T(8,128)(2,1)} %fusion.14) | copy-start | bytes 1179652
  190.8 12.0 %copy-start.16 = (f32[20,32,128]{2,1,0:T(8,128)S(1)}, f32[20,32,128]{2,1,0:T(8,128)}, u32[]{:S(2)}) copy-start(f32[20,32,128]{2,1,0:T(8,128)} %copy.78) | copy-start | bytes 983044
  190.8 12.0 %copy-start.17 = (f32[20,32,34]{2,1,0:T(8,128)S(1)}, f32[20,32,34]{2,1,0:T(8,128)}, u32[]{:S(2)}) copy-start(f32[20,32,34]{2,1,0:T(8,128)} %convolution_bitcast_fusion.2) | copy-start | bytes 261124
  190.8 12.0 %copy-start.25 = (s32[128]{0:T(128)S(1)}, s32[128]{0:T(128)}, u32[]{:S(2)}) copy-start(s32[128]{0:T(128)} %get-tuple-element.30) | copy-start | bytes 1540
  190.8 12.0 %copy-start.26 = (s32[128]{0:T(128)S(1)}, s32[128]{0:T(128)}, u32[]{:S(2)}) copy-start(s32[128]{0:T(128)} %get-tuple-element.31) | copy-start | bytes 1540
  190.8 12.1 %copy-start.27 = (f32[128]{0:T(128)S(1)}, f32[128]{0:T(128)}, u32[]{:S(2)}) copy-start(f32[128]{0:T(128)} %get-tuple-element.24) | copy-start | bytes 1540
  190.8 12.0 %copy-start.28 = (f32[128]{0:T(128)S(1)}, f32[128]{0:T(128)}, u32[]{:S(2)}) copy-start(f32[128]{0:T(128)} %get-tuple-element.25) | copy-start | bytes 1540
  193.4 17.3 %collective-permute-start.4 = (f32[8,8,1536]{2,1,0:T(8,128)}, f32[8,8,1536]{2,1,0:T(8,128)S(1)}, u32[]{:S(2)}, u32[]{:S(2)}) collective-permute-start(f32[8,8,1536]{2,1,0:T(8,128)} %get-tuple-element.9), channel_id=1, source_target_pairs={{0,1},{1,2},{2,3},{3,4},{4,5},{5,6},{6,7},{7,8},{8,9},{9,10},{10,1... | collective-permute-start | bytes 1179656 | tf_op jit(solution)/shard_map/ppermute | solution.py:33
  195.3 16.7 %collective-permute-start.5 = (f32[8,8,1536]{2,1,0:T(8,128)}, f32[8,8,1536]{2,1,0:T(8,128)}, u32[]{:S(2)}, u32[]{:S(2)}) collective-permute-start(f32[8,8,1536]{2,1,0:T(8,128)} %get-tuple-element.10), channel_id=1, source_target_pairs={{0,15},{1,0},{2,1},{3,2},{4,3},{5,4},{6,5},{7,6},{8,7},{9,8},{10,9... | collective-permute-start | bytes 1179656 | tf_op jit(solution)/shard_map/ppermute | solution.py:33
  205.4 6.6 %copy-start.7 = (f32[8,48,1536]{2,1,0:T(8,128)S(1)}, f32[8,48,1536]{2,1,0:T(8,128)}, u32[]{:S(2)}) copy-start(f32[8,48,1536]{2,1,0:T(8,128)} %copy-done.6) | copy-start | bytes 7077892
  206.4 16.9 %all-to-all-start = ((bf16[16,8,6,320]{3,1,2,0:T(8,128)(2,1)}), bf16[16,8,6,320]{3,1,2,0:T(8,128)(2,1)}, u32[]{:S(2)}, u32[]{:S(2)}) async-start(bf16[16,8,6,320]{3,1,2,0:T(8,128)(2,1)} %bitcast.121), calls=%async_computation | async-start | bytes 1179648 | tf_op jit(solution)/shard_map/all_to_all | solution.py:159
  210.7 22.2 %copy-start.24 = (f32[1536]{0:T(1024)S(1)}, f32[1536]{0:T(1024)}, u32[]{:S(2)}) copy-start(f32[1536]{0:T(1024)} %param.8) | copy-start | bytes 18436
  225.2 23.3 %all-to-all-start.1 = ((f32[16,6,320]{2,1,0:T(8,128)}), f32[16,6,320]{2,1,0:T(8,128)S(1)}, u32[]{:S(2)}, u32[]{:S(2)}) async-start(f32[16,6,320]{2,1,0:T(8,128)} %bitcast.39), calls=%async_computation.1 | async-start | bytes 393216 | tf_op jit(solution)/shard_map/all_to_all | solution.py:162
  232.9 19.9 %copy-start.4 = (f32[256,1536]{1,0:T(8,128)S(1)}, f32[256,1536]{1,0:T(8,128)}, u32[]{:S(2)}) copy-start(f32[256,1536]{1,0:T(8,128)} %copy-done.3) | copy-start | bytes 4718596
  249.2 11.8 %all-to-all-start.2 = ((f32[16,6,320]{2,1,0:T(8,128)}), f32[16,6,320]{2,1,0:T(8,128)S(1)}, u32[]{:S(2)}, u32[]{:S(2)}) async-start(f32[16,6,320]{2,1,0:T(8,128)} %broadcast_in_dim.80), calls=%async_computation.2 | async-start | bytes 393216 | tf_op jit(solution)/shard_map/all_to_all | solution.py:165
  252.8 9.0 %copy-start.1 = (bf16[96,2304]{1,0:T(8,128)(2,1)S(1)}, bf16[96,2304]{1,0:T(8,128)(2,1)}, u32[]{:S(2)}) copy-start(bf16[96,2304]{1,0:T(8,128)(2,1)} %param.9) | copy-start | bytes 1327108
  (8 other events, 14.0 us)
Sparse Core Ops, SparseCore 0:
  10.7 86.5 all-gather.1
where the time goes:
time: 270 us; the launch traced here: 269 us
  waiting for transfers between devices  95.1 us (35%)
  local copies, waits for them, and re-layouts  67.9 us (25%)
  starting transfers between devices  45.3 us (17%)
  matrix products  33.3 us (12%)
  between operations  14.6 us (5%)
  other arithmetic  12.4 us (5%)
    all_gather x1, waiting for transfers between devices, gather_weights(): full = lax.all_gather(packed, ('dp',) + FSDP, axis=0, tiled=True)  70.3 us
    ppermute x2, starting transfers between devices, with_halo(): after = lax.ppermute(leading, axis, down)  11.7 us
    dot_general x3, matrix products, contract_last(): lax.dot_general(left_side, right_side, (((1,), (1,)), ((), ())), preferre...  10.5 us
    ppermute x2, starting transfers between devices, from_behind(): return lax.ppermute(value, axis, pairs)  9.37 us
    all_to_all x1, waiting for transfers between devices, reduce_head(): pieces = lax.all_to_all(pieces, TILE, 0, 0, tiled=True)  9.29 us
    unnamed x61, local copies, waits for them, and re-layouts  9.08 us
    all_to_all x1, waiting for transfers between devices, reduce_head(): both = lax.all_to_all(both, ('dp', 'z'), 0, 0, tiled=True)  8.76 us
    all_to_all x1, starting transfers between devices, reduce_head(): both = lax.all_to_all(both, ('dp', 'z'), 0, 0, tiled=True)  7.69 us
  transfers between devices with their start and end apart: 11, of which 5 were waited for; matrix products, arithmetic and copies ran while one was open for 19% of the time, Pallas kernels for 0%

commit v1 on v0

--- a/solution.py
+++ b/solution.py
@@ -12,6 +12,13 @@
 INNER = 768
 HEAD_OUT = 320
 EPSILON = 1e-05
+
+
+def gather_over(value, name, dim):
+    count = lax.axis_size(name)
+    tiles = jnp.stack([value for _ in range(count)])
+    tiles = lax.all_to_all(tiles, name, split_axis=0, concat_axis=0)
+    return jnp.concatenate(tiles, axis=dim)
 
 
 def with_halo(shard, sides, width):
@@ -140,7 +147,7 @@
     out_half = jnp.concatenate([out_half[:, :384], out_half[:, 384:]], axis=0)
     head_half = lax.dynamic_slice_in_dim(head_w, half * 160, 160, 1)
     packed = jnp.concatenate([qkv_half, out_half, head_half], axis=1)
-    full = lax.all_gather(packed, ("dp",) + FSDP, axis=0, tiled=True)
+    full = gather_over(packed, ("dp",) + FSDP, 0)
     full = full.reshape(2, D, 1696)
     full_qkv = jnp.concatenate([full[0, :, :HALF_QKV], full[1, :, :HALF_QKV]], axis=1)
     out_part = full[:, :, HALF_QKV:1536].reshape(2, 16, 2, 48, 384)

time: 270 us -> 659 us (2.44)
  waiting for transfers between devices: 95.1 us -> 491 us
  between operations: 14.6 us -> 1.2 us
  starting transfers between devices: 45.3 us -> 57.3 us
    all_to_all x0 -> x1, waiting for transfers between devices: none -> 466 us  [gather_over(): tiles = lax.all_to_all(tiles, name, split_axis=0, concat_axis=0)]
    all_gather x1 -> x0, waiting for transfers between devices: 70.3 us -> none  [gather_weights(): full = lax.all_gather(packed, ('dp',) + FSDP, axis=0, tiled=True)]
    all_to_all x0 -> x1, starting transfers between devices: none -> 15.4 us  [gather_over(): tiles = lax.all_to_all(tiles, name, split_axis=0, concat_axis=0)]
  transfers between devices with their start and end apart: 11 -> 11, of which waited for: 5 -> 6; matrix products, arithmetic and copies ran while one was open for 19% -> 7% of each run, Pallas kernels for 0% -> 0%
where the time goes in v1:
time: 659 us; the launch traced here: 658 us
  waiting for transfers between devices  491 us (75%)
  local copies, waits for them, and re-layouts  67.3 us (10%)
  starting transfers between devices  57.3 us (9%)
  matrix products  31.4 us (5%)
  other arithmetic  9.95 us (2%)
    all_to_all x1, waiting for transfers between devices, gather_over(): tiles = lax.all_to_all(tiles, name, split_axis=0, concat_axis=0)  466 us
    all_to_all x1, starting transfers between devices, gather_over(): tiles = lax.all_to_all(tiles, name, split_axis=0, concat_axis=0)  15.4 us
  transfers between devices with their start and end apart: 11, of which 6 were waited for; matrix products, arithmetic and copies ran while one was open for 7% of the time, Pallas kernels for 0%

profile of v1, /device:TPU:32, one launch (start us, length us, event | category | flops | bytes accessed | tf_op | source)
XLA Modules:
  0.0 657.8 jit_solution(6848611531822275728)
XLA Ops:
  2.6 5.3 stack.2
  7.9 15.4 %all-to-all-start = ((bf16[32,96,1696]{2,1,0:T(8,128)(2,1)}), bf16[32,96,1696]{2,1,0:T(8,128)(2,1)}, u32[]{:S(2)}, u32[]{:S(2)}) async-start(bf16[32,96,1696]{2,1,0:T(8,128)(2,1)} %stack.2), calls=%async_computation | async-start | bytes 22020096 | tf_op jit(solution)/shard_map/all_to_all | solution.py:20
  23.4 3.4 collective-permute-start.2
  26.8 5.8 collective-permute-start.3
  37.9 466.3 %all-to-all-done = bf16[32,96,1696]{2,1,0:T(8,128)(2,1)} async-done(((bf16[32,96,1696]{2,1,0:T(8,128)(2,1)}), bf16[32,96,1696]{2,1,0:T(8,128)(2,1)}, u32[]{:S(2)}, u32[]{:S(2)}) %all-to-all-start) | async-done | bytes 10420256 | tf_op jit(solution)/shard_map/all_to_all | solution.py:20
  504.3 2.7 slice_bitcast_fusion.3
  508.8 3.6 slice_bitcast_fusion.1
  512.5 3.8 fusion.3
  517.2 3.7 copy.76
  520.9 5.3 reshape.210
  528.2 3.4 collective-permute-start
  531.6 5.9 collective-permute-start.1
  548.5 2.9 fusion.68
  551.4 2.9 convolution_convert_fusion.1
  562.3 2.4 copy.85
  571.9 3.1 copy.77
  575.0 2.3 copy.78
  577.2 3.0 copy.83
  580.2 2.8 concatenate.36
  584.0 3.0 copy.82
  587.0 2.7 concatenate.35
  595.8 7.5 %collective-permute-start.5 = (f32[8,8,1536]{2,1,0:T(8,128)}, f32[8,8,1536]{2,1,0:T(8,128)}, u32[]{:S(2)}, u32[]{:S(2)}) collective-permute-start(f32[8,8,1536]{2,1,0:T(8,128)} %get-tuple-element.10), channel_id=1, source_target_pairs={{0,15},{1,0},{2,1},{3,2},{4,3},{5,4},{6,5},{7,6},{8,7},{9,8},{10,9... | collective-permute-start | bytes 1179656 | tf_op jit(solution)/shard_map/ppermute | solution.py:40
  606.9 3.6 all-to-all-start.1
  610.9 3.7 collective-permute-done.5
  614.6 2.5 fusion.10
  617.0 6.0 all-to-all-done.1
  623.9 5.0 all-to-all-start.2
  628.9 6.8 %fusion.63 = (f32[256]{0:T(256)S(1)}, f32[256]{0:T(256)S(1)}, f32[256,1536]{1,0:T(8,128)}) fusion(f32[256]{0:T(256)S(1)} %rsqrt.12, f32[256]{0:T(256)S(1)} %div.51, bf16[1,8,32,1536]{3,2,1,0:T(8,128)(2,1)S(1)} %copy-done.4, f32[1536]{0:T(1024)S(1)} %copy-done.23, bf16[1536,1152]{1,0:T(8,128)(2,1)} %copy-done.11, bf16[1536,1152]{1,0:T(8,128)(2,1)} %copy-done.10, ...), kind=kOutput, calls=%fused_computation.128 | convolution fusion | flops 1831206400 | bytes 10627072 | tf_op jit(solution)/shard_map/dot_general | solution.py:128
  635.8 8.7 %all-to-all-done.2 = f32[16,6,320]{2,1,0:T(8,128)S(1)} async-done(((f32[16,6,320]{2,1,0:T(8,128)}), f32[16,6,320]{2,1,0:T(8,128)S(1)}, u32[]{:S(2)}, u32[]{:S(2)}) %all-to-all-start.2) | async-done | bytes 122912 | tf_op jit(solution)/shard_map/all_to_all | solution.py:169
  645.2 3.5 all-to-all-start.3
  648.8 2.9 add_convert_fusion
  651.7 5.4 all-to-all-done.3
  (114 shorter events, 51.3 us)
Async XLA Ops:
  0.6 1.9 copy-start
  7.9 15.5 %copy-start.17 = (f32[1,20,8,32]{3,2,1,0:T(8,128)S(1)}, f32[1,20,8,32]{3,2,1,0:T(8,128)}, u32[]{:S(2)}) copy-start(f32[1,20,8,32]{3,2,1,0:T(8,128)} %param.12) | copy-start | bytes 61444
  7.9 24.7 %copy-start.20 = (f32[1,20,32,128]{3,2,1,0:T(8,128)S(1)}, f32[1,20,32,128]{3,2,1,0:T(8,128)}, u32[]{:S(2)}) copy-start(f32[1,20,32,128]{3,2,1,0:T(8,128)} %param.13) | copy-start | bytes 983044
  7.9 496.4 %all-to-all-start = ((bf16[32,96,1696]{2,1,0:T(8,128)(2,1)}), bf16[32,96,1696]{2,1,0:T(8,128)(2,1)}, u32[]{:S(2)}, u32[]{:S(2)}) async-start(bf16[32,96,1696]{2,1,0:T(8,128)(2,1)} %stack.2), calls=%async_computation | async-start | bytes 22020096 | tf_op jit(solution)/shard_map/all_to_all | solution.py:20
  23.4 13.2 %collective-permute-start.2 = (f32[20,8,1]{2,1,0:T(8,128)S(1)}, f32[20,8,1]{2,1,0:T(8,128)S(1)}, u32[]{:S(2)}, u32[]{:S(2)}) collective-permute-start(f32[20,8,1]{2,1,0:T(8,128)S(1)} %get-tuple-element.17), channel_id=1, source_target_pairs={{0,1},{1,2},{2,3},{3,4},{4,5},{5,6},{6,7},{7,8},{8,9},{9,10},{10,1... | collective-permute-start | bytes 1928 | tf_op jit(solution)/shard_map/ppermute | solution.py:31
  26.8 9.9 %collective-permute-start.3 = (f32[20,8,1]{2,1,0:T(8,128)S(1)}, f32[20,8,1]{2,1,0:T(8,128)S(1)}, u32[]{:S(2)}, u32[]{:S(2)}) collective-permute-start(f32[20,8,1]{2,1,0:T(8,128)S(1)} %get-tuple-element.18), channel_id=1, source_target_pairs={{1,0},{2,1},{3,2},{4,3},{5,4},{6,5},{7,6},{8,7},{9,8},{10,9},{11,1... | collective-permute-start | bytes 1928 | tf_op jit(solution)/shard_map/ppermute | solution.py:32
  33.2 2.4 copy-start.2
  34.7 1.7 copy-start.23
  35.9 593.0 %copy-start.21 = (f32[256]{0:T(256)}, f32[256]{0:T(256)S(1)}, u32[]{:S(2)}) copy-start(f32[256]{0:T(256)S(1)} %div.51) | copy-start | bytes 3076
  36.3 592.6 %copy-start.22 = (f32[256]{0:T(256)}, f32[256]{0:T(256)S(1)}, u32[]{:S(2)}) copy-start(f32[256]{0:T(256)S(1)} %rsqrt.12) | copy-start | bytes 3076
  512.4 3.8 copy-start.10
  512.5 3.8 copy-start.11
  528.2 14.4 %collective-permute-start = (bf16[8,8,1536]{2,1,0:T(8,128)(2,1)}, bf16[8,8,1536]{2,1,0:T(8,128)(2,1)}, u32[]{:S(2)}, u32[]{:S(2)}) collective-permute-start(bf16[8,8,1536]{2,1,0:T(8,128)(2,1)} %get-tuple-element.13), channel_id=1, source_target_pairs={{0,1},{1,2},{2,3},{3,4},{4,5},{5,6},{6,7},{7,8},{8,9},{9,10},{10,1... | collective-permute-start | bytes 589832 | tf_op jit(solution)/shard_map/ppermute | solution.py:31
  531.6 11.0 %collective-permute-start.1 = (bf16[8,8,1536]{2,1,0:T(8,128)(2,1)}, bf16[8,8,1536]{2,1,0:T(8,128)(2,1)}, u32[]{:S(2)}, u32[]{:S(2)}) collective-permute-start(bf16[8,8,1536]{2,1,0:T(8,128)(2,1)} %get-tuple-element.14), channel_id=1, source_target_pairs={{1,0},{2,1},{3,2},{4,3},{5,4},{6,5},{7,6},{8,7},{9,8},{10,9},{11,1... | collective-permute-start | bytes 589832 | tf_op jit(solution)/shard_map/ppermute | solution.py:32
  551.4 3.0 copy-start.7
  551.4 3.1 copy-start.19
  554.4 1.6 copy-start.18
  566.4 3.1 copy-start.12
  566.4 3.1 copy-start.13
  566.4 3.1 copy-start.14
  567.5 36.9 %collective-permute-start.6 = (f32[8,96,320]{2,1,0:T(8,128)}, f32[8,96,320]{2,1,0:T(8,128)}, u32[]{:S(2)}, u32[]{:S(2)}) collective-permute-start(f32[8,96,320]{2,1,0:T(8,128)} %dynamic-slice_bitcast_fusion), channel_id=1, source_target_pairs={{0,16},{16,0},{1,17},{17,1},{2,18},{18,2},{3,19},{19,3},{4,20},{20... | collective-permute-start | bytes 2949128 | tf_op jit(solution)/shard_map/ppermute | solution.py:164
  580.2 2.8 copy-start.15
  589.7 1.6 copy-start.9
  591.3 12.0 %copy-start.16 = (f32[20,32,34]{2,1,0:T(8,128)S(1)}, f32[20,32,34]{2,1,0:T(8,128)}, u32[]{:S(2)}) copy-start(f32[20,32,34]{2,1,0:T(8,128)} %convolution_bitcast_fusion.2) | copy-start | bytes 261124
  593.9 16.9 %collective-permute-start.4 = (f32[8,8,1536]{2,1,0:T(8,128)}, f32[8,8,1536]{2,1,0:T(8,128)S(1)}, u32[]{:S(2)}, u32[]{:S(2)}) collective-permute-start(f32[8,8,1536]{2,1,0:T(8,128)} %get-tuple-element.9), channel_id=1, source_target_pairs={{0,1},{1,2},{2,3},{3,4},{4,5},{5,6},{6,7},{7,8},{8,9},{9,10},{10,1... | collective-permute-start | bytes 1179656 | tf_op jit(solution)/shard_map/ppermute | solution.py:40
  595.8 18.7 %collective-permute-start.5 = (f32[8,8,1536]{2,1,0:T(8,128)}, f32[8,8,1536]{2,1,0:T(8,128)}, u32[]{:S(2)}, u32[]{:S(2)}) collective-permute-start(f32[8,8,1536]{2,1,0:T(8,128)} %get-tuple-element.10), channel_id=1, source_target_pairs={{0,15},{1,0},{2,1},{3,2},{4,3},{5,4},{6,5},{7,6},{8,7},{9,8},{10,9... | collective-permute-start | bytes 1179656 | tf_op jit(solution)/shard_map/ppermute | solution.py:40
  606.9 16.2 %all-to-all-start.1 = ((bf16[16,8,6,320]{3,1,2,0:T(8,128)(2,1)}), bf16[16,8,6,320]{3,1,2,0:T(8,128)(2,1)S(1)}, u32[]{:S(2)}, u32[]{:S(2)}) async-start(bf16[16,8,6,320]{3,1,2,0:T(8,128)(2,1)} %bitcast.38), calls=%async_computation.1 | async-start | bytes 1179648 | tf_op jit(solution)/shard_map/all_to_all | solution.py:166
  610.5 18.4 %copy-start.4 = (bf16[1,8,32,1536]{3,2,1,0:T(8,128)(2,1)S(1)}, bf16[1,8,32,1536]{3,2,1,0:T(8,128)(2,1)}, u32[]{:S(2)}) copy-start(bf16[1,8,32,1536]{3,2,1,0:T(8,128)(2,1)} %param.7) | copy-start | bytes 2359300
  623.9 20.6 %all-to-all-start.2 = ((f32[16,6,320]{2,1,0:T(8,128)}), f32[16,6,320]{2,1,0:T(8,128)S(1)}, u32[]{:S(2)}, u32[]{:S(2)}) async-start(f32[16,6,320]{2,1,0:T(8,128)} %bitcast.39), calls=%async_computation.2 | async-start | bytes 393216 | tf_op jit(solution)/shard_map/all_to_all | solution.py:169
  628.9 19.9 %copy-start.6 = (f32[256,1536]{1,0:T(8,128)S(1)}, f32[256,1536]{1,0:T(8,128)}, u32[]{:S(2)}) copy-start(f32[256,1536]{1,0:T(8,128)} %copy-done.5) | copy-start | bytes 4718596
  645.2 11.8 %all-to-all-start.3 = ((f32[16,6,320]{2,1,0:T(8,128)}), f32[16,6,320]{2,1,0:T(8,128)S(1)}, u32[]{:S(2)}, u32[]{:S(2)}) async-start(f32[16,6,320]{2,1,0:T(8,128)} %broadcast_in_dim.80), calls=%async_computation.3 | async-start | bytes 393216 | tf_op jit(solution)/shard_map/all_to_all | solution.py:172
  648.8 9.0 %copy-start.1 = (bf16[96,2304]{1,0:T(8,128)(2,1)S(1)}, bf16[96,2304]{1,0:T(8,128)(2,1)}, u32[]{:S(2)}) copy-start(bf16[96,2304]{1,0:T(8,128)(2,1)} %param.9) | copy-start | bytes 1327108
  (3 other events, 4.1 us)
